TPU v7x, 32 devices: a whole 2x2x4 slice. The times are simulated.
32 devices in a mesh: pipe: 2 (over x), dp: 4 (over y, core), tensor: 4 (over z).
Axes of the slice: x: 2, y: 2, z: 4, core: 2. Of those that a mesh axis runs over, the one named last changes fastest.
Arguments:
- inputs: bfloat16 [4, 1024, 1024], P(None, ('dp', 'tensor')), may hold values from -6 to 6
- segments: int32 [4, 1024], P(None, 'dp'), may hold values from 0 to 7, never falling along the last dimension, each value on 1 to 256 neighbouring positions
- cotangent: bfloat16 [4, 1024, 1024], P(None, ('dp', 'tensor')), may hold values from -6 to 6
- w_qkv: bfloat16 [2, 1024, 3, 1024], P('pipe', 'dp', None, 'tensor'), may hold values from -0.1875 to 0.1875
- w_o: bfloat16 [2, 1024, 1024], P('pipe', 'tensor', 'dp'), may hold values from -1.5 to 1.5
- w_in: bfloat16 [2, 1024, 4096], P('pipe', 'dp', 'tensor'), may hold values from -0.1875 to 0.1875
- w_out: bfloat16 [2, 4096, 1024], P('pipe', 'tensor', 'dp'), may hold values from -0.09375 to 0.09375
- ln_gains: float32 [2, 2, 1024], P('pipe'), may hold values from 0.1 to 1.9
- model_biases: float32 [2, 6, 1024], P('pipe'), may hold values from -1 to 1
- hidden_bias: float32 [2, 4096], P('pipe'), may hold values from -2.5 to 2.5
Outputs:
- section_outputs: bfloat16 [2, 4, 1024, 1024], P('pipe', None, ('dp', 'tensor'))
- input_grads: bfloat16 [2, 4, 1024, 1024], P('pipe', None, ('dp', 'tensor'))
- grad_qkv: float32 [2, 1024, 3, 1024], P('pipe', 'dp', None, 'tensor')
- grad_o: float32 [2, 1024, 1024], P('pipe', 'tensor', 'dp')
- grad_in: float32 [2, 1024, 4096], P('pipe', 'dp', 'tensor')
- grad_out: float32 [2, 4096, 1024], P('pipe', 'tensor', 'dp')
- grad_gains: float32 [2, 2, 1024], P('pipe', None, ('dp', 'tensor'))
- grad_biases: float32 [2, 6, 1024], P('pipe', None, ('dp', 'tensor'))
- grad_hidden_bias: float32 [2, 4096], P('pipe', ('dp', 'tensor'))
Inputs may be any that keep to these rules, and one draw needn't show every extreme that they name: `segments`: segment numbers never fall along a micro-batch's 1024 tokens; a segment holds 1 to 256 tokens and some segment holds exactly 256.
All inputs are finite; a program needn't handle non-finite values.
Results may differ from a plain program's by a relative error of at most 0.028.
Values may be sent and summed in bfloat16 or wider, within the bound.
No kernel may reach another device: no remote copies, remote signals or barrier semaphores. Data moves between devices by JAX's collectives and lax.ppermute only.
A program may use at most 128 MiB of HBM per device.

v0:
```python
import jax
import jax.numpy as jnp
from jax import lax
from jax.sharding import PartitionSpec as P

HEAD_DIM = 64
NORM_EPS = 1e-12
MASKED = -1000000000.0
ROOT_HALF = 0.7071067811865476
INV_ROOT_TWOPI = 0.3989422804014327


def shifted(block, axis, distance):
    devices = range(lax.axis_size(axis))
    route = [(i - distance, i) for i in devices if i - distance in devices]
    return lax.ppermute(block, axis, route)


def dot_rows(left_side, right_side):
    return lax.dot_general(
        left_side, right_side, (((0,), (0,)), ((), ())), preferred_element_type=jnp.float32
    )


def dot_cols(left_side, right_side):
    return lax.dot_general(
        left_side, right_side, (((1,), (1,)), ((), ())), preferred_element_type=jnp.float32
    )


def norm_forward(values, gain_row, shift_row):
    center = values - jnp.mean(values, axis=-1, keepdims=True)
    spread = jnp.mean(center * center, axis=-1, keepdims=True)
    inverse = lax.rsqrt(spread + NORM_EPS)
    scaled = center * inverse
    return (scaled * gain_row + shift_row, scaled, inverse)


def norm_backward(upstream, scaled, inverse, gain_row):
    weighted = upstream * gain_row
    inner_term = (
        weighted
        - jnp.mean(weighted, axis=-1, keepdims=True)
        - scaled * jnp.mean(weighted * scaled, axis=-1, keepdims=True)
    )
    return (inverse * inner_term, jnp.sum(upstream * scaled, axis=0), jnp.sum(upstream, axis=0))


def gelu_slope(values):
    return 0.5 * (1.0 + lax.erf(values * ROOT_HALF)) + values * INV_ROOT_TWOPI * jnp.exp(
        -0.5 * values * values
    )


def masked_scores(query_seq, key_seq, label_seq):
    scores = jnp.einsum(
        "qhe,khe->hqk", query_seq, key_seq, preferred_element_type=jnp.float32
    ) * HEAD_DIM ** (-0.5)
    allowed = label_seq[:, None] == label_seq[None, :]
    return jnp.where(allowed[None], scores, MASKED)


def attend(queries, key_rows, value_rows, labels):
    row_count, local_width = queries.shape
    heads_here = local_width // HEAD_DIM
    shaped = [
        member.reshape(1, row_count, heads_here, HEAD_DIM)
        for member in (queries, key_rows, value_rows)
    ]

    def one_sequence(pieces):
        query_seq, key_seq, value_seq, label_seq = pieces
        scores = masked_scores(query_seq, key_seq, label_seq)
        largest = jnp.max(scores, axis=-1, keepdims=True)
        total_mass = jnp.sum(jnp.exp(scores - largest), axis=-1, keepdims=True)
        log_total = largest + jnp.log(total_mass)
        weights = jnp.exp(scores - log_total).astype(jnp.bfloat16)
        context = jnp.einsum("hqk,khe->qhe", weights, value_seq, preferred_element_type=jnp.float32)
        return (context.astype(jnp.bfloat16), log_total[..., 0])

    context, log_total = lax.map(
        one_sequence, (shaped[0], shaped[1], shaped[2], labels.reshape(1, row_count))
    )
    return (context.reshape(row_count, local_width), log_total)


def attend_back(queries, key_rows, value_rows, labels, log_total, grad_context):
    row_count, local_width = queries.shape
    heads_here = local_width // HEAD_DIM
    shaped = [
        member.reshape(1, row_count, heads_here, HEAD_DIM)
        for member in (queries, key_rows, value_rows, grad_context)
    ]
    score_scale = HEAD_DIM ** (-0.5)

    def one_sequence(pieces):
        query_seq, key_seq, value_seq, label_seq, total_seq, grad_seq = pieces
        scores = masked_scores(query_seq, key_seq, label_seq)
        weights = jnp.exp(scores - total_seq[..., None])
        weights_low = weights.astype(jnp.bfloat16)
        grad_weights = jnp.einsum(
            "qhe,khe->hqk", grad_seq, value_seq, preferred_element_type=jnp.float32
        )
        inner_term = jnp.sum(weights * grad_weights, axis=-1, keepdims=True)
        grad_scores = (weights * (grad_weights - inner_term)).astype(jnp.bfloat16)
        grad_query = (
            jnp.einsum("hqk,khe->qhe", grad_scores, key_seq, preferred_element_type=jnp.float32)
            * score_scale
        )
        grad_keys = (
            jnp.einsum("hqk,qhe->khe", grad_scores, query_seq, preferred_element_type=jnp.float32)
            * score_scale
        )
        grad_values = jnp.einsum(
            "hqk,qhe->khe", weights_low, grad_seq, preferred_element_type=jnp.float32
        )
        return jnp.stack((grad_query, grad_keys, grad_values), axis=1).astype(jnp.bfloat16)

    stacked = lax.map(
        one_sequence,
        (shaped[0], shaped[1], shaped[2], labels.reshape(1, row_count), log_total, shaped[3]),
    )
    return stacked.reshape(row_count, 3, local_width)


def layer_forward(current, labels, weights, vectors):
    w_qkv, w_o, w_in, w_out = weights
    gains, biases, query_bias, value_bias, local_hidden_bias = vectors
    gathered = lax.all_gather(current, "tensor", axis=0, tiled=True)
    projected = jnp.einsum("gd,dcn->gcn", gathered, w_qkv, preferred_element_type=jnp.float32)
    queries = (projected[:, 0] + query_bias).astype(jnp.bfloat16)
    key_rows = projected[:, 1].astype(jnp.bfloat16)
    value_rows = (projected[:, 2] + value_bias).astype(jnp.bfloat16)
    context, log_total = attend(queries, key_rows, value_rows, labels)
    partial_value = jnp.dot(context, w_o, preferred_element_type=jnp.float32)
    mixed_rows = lax.psum_scatter(partial_value, "tensor", scatter_dimension=0, tiled=True)
    normed, scaled_one, inverse_one = norm_forward(
        current.astype(jnp.float32) + mixed_rows + biases[2], gains[0], biases[3]
    )
    spread_rows = lax.all_gather(normed.astype(jnp.bfloat16), "tensor", axis=0, tiled=True)
    hidden = jnp.dot(spread_rows, w_in, preferred_element_type=jnp.float32) + local_hidden_bias
    active = jax.nn.gelu(hidden, approximate=False).astype(jnp.bfloat16)
    partial_out = jnp.dot(active, w_out, preferred_element_type=jnp.float32)
    branch = lax.psum_scatter(
        partial_out.astype(jnp.bfloat16), "tensor", scatter_dimension=0, tiled=True
    ).astype(jnp.float32)
    final_rows, scaled_two, inverse_two = norm_forward(
        normed + branch + biases[4], gains[1], biases[5]
    )
    kept_state = (
        gathered,
        queries,
        key_rows,
        value_rows,
        context,
        log_total,
        scaled_one,
        inverse_one,
        spread_rows,
        hidden,
        active,
        scaled_two,
        inverse_two,
    )
    return (final_rows.astype(jnp.bfloat16), kept_state)


def layer_backward(upstream, kept_state, labels, weights, gains):
    (
        gathered,
        queries,
        key_rows,
        value_rows,
        context,
        log_total,
        scaled_one,
        inverse_one,
        spread_rows,
        hidden,
        active,
        scaled_two,
        inverse_two,
    ) = kept_state
    w_qkv, w_o, w_in, w_out = weights
    grad_second, gain_two, shift_two = norm_backward(upstream, scaled_two, inverse_two, gains[1])
    grad_feed = lax.all_gather(grad_second.astype(jnp.bfloat16), "tensor", axis=0, tiled=True)
    grad_active = dot_cols(grad_feed, w_out)
    grad_w_out = dot_rows(active, grad_feed)
    grad_hidden = (grad_active * gelu_slope(hidden)).astype(jnp.bfloat16)
    grad_w_in = dot_rows(spread_rows, grad_hidden)
    grad_spread = dot_cols(grad_hidden, w_in)
    grad_normed = grad_second + lax.psum_scatter(
        grad_spread.astype(jnp.bfloat16), "tensor", scatter_dimension=0, tiled=True
    ).astype(jnp.float32)
    grad_first, gain_one, shift_one = norm_backward(grad_normed, scaled_one, inverse_one, gains[0])
    grad_mix = lax.all_gather(grad_first.astype(jnp.bfloat16), "tensor", axis=0, tiled=True)
    grad_context = dot_cols(grad_mix, w_o).astype(jnp.bfloat16)
    grad_w_o = dot_rows(context, grad_mix)
    grad_project = attend_back(queries, key_rows, value_rows, labels, log_total, grad_context)
    grad_w_qkv = jnp.einsum(
        "gd,gcn->dcn", gathered, grad_project, preferred_element_type=jnp.float32
    )
    grad_gathered = jnp.einsum(
        "gcn,dcn->gd", grad_project, w_qkv, preferred_element_type=jnp.float32
    )
    grad_current = grad_first + lax.psum_scatter(
        grad_gathered.astype(jnp.bfloat16), "tensor", scatter_dimension=0, tiled=True
    ).astype(jnp.float32)
    column_sums = jnp.sum(grad_project.astype(jnp.float32), axis=0)
    gain_grads = jnp.stack([gain_one, gain_two])
    row_grads = jnp.stack(
        [jnp.sum(grad_first, axis=0), shift_one, jnp.sum(grad_second, axis=0), shift_two]
    )
    local_grads = jnp.stack([column_sums[0], column_sums[2]])
    hidden_grads = jnp.sum(grad_hidden.astype(jnp.float32), axis=0)
    return (
        grad_current,
        (grad_w_qkv, grad_w_o, grad_w_in, grad_w_out),
        (gain_grads, row_grads, local_grads, hidden_grads),
    )


def body(inputs, segments, cotangent, w_qkv, w_o, w_in, w_out, ln_gains, model_biases, hidden_bias):
    section_first = lax.axis_index("pipe") == 0
    column = lax.axis_index("tensor")
    micro_count = inputs.shape[0]
    row_count = inputs.shape[1]
    model_width = model_biases.shape[-1]
    hidden_width = hidden_bias.shape[-1]
    width_local = w_qkv.shape[-1]
    hidden_local = w_in.shape[-1]
    gains = ln_gains[0]
    biases = model_biases[0]
    query_bias = lax.dynamic_slice_in_dim(biases[0], column * width_local, width_local)
    value_bias = lax.dynamic_slice_in_dim(biases[1], column * width_local, width_local)
    local_hidden_bias = lax.dynamic_slice_in_dim(
        hidden_bias[0], column * hidden_local, hidden_local
    )
    vectors = (gains, biases, query_bias, value_bias, local_hidden_bias)
    shards = (w_qkv[0], w_o[0], w_in[0], w_out[0])
    blank_rows = jnp.zeros((row_count, model_width), jnp.bfloat16)
    incoming = blank_rows
    returning = blank_rows
    kept_list = []
    forward_list = []
    backward_list = []
    weight_totals = None
    vector_totals = None
    for tick_index in range(micro_count + 2):
        weights = (
            lax.all_gather(shards[0], "dp", axis=0, tiled=True),
            lax.all_gather(shards[1], "dp", axis=1, tiled=True),
            lax.all_gather(shards[2], "dp", axis=0, tiled=True),
            lax.all_gather(shards[3], "dp", axis=1, tiled=True),
        )
        own_rows = inputs[tick_index] if tick_index < micro_count else blank_rows
        current = jnp.where(section_first, own_rows, incoming)
        labels_forward = jnp.where(
            section_first,
            segments[min(tick_index, micro_count - 1)],
            segments[max(min(tick_index - 1, micro_count - 1), 0)],
        )
        final_rows, kept_state = layer_forward(current, labels_forward, weights, vectors)
        forward_list.append(final_rows)
        incoming = shifted(final_rows, "pipe", 1)
        given_grad = cotangent[tick_index - 1] if 1 <= tick_index <= micro_count else blank_rows
        upstream = jnp.where(section_first, returning, given_grad).astype(jnp.float32)
        earlier = kept_list[tick_index - 2] if tick_index >= 2 else kept_state
        chosen_state = jax.tree.map(
            lambda first_item, second_item: jnp.where(section_first, first_item, second_item),
            earlier,
            kept_state,
        )
        labels_backward = jnp.where(
            section_first,
            segments[max(min(tick_index - 2, micro_count - 1), 0)],
            segments[max(min(tick_index - 1, micro_count - 1), 0)],
        )
        grad_current, weight_grads, vector_grads = layer_backward(
            upstream, chosen_state, labels_backward, weights, gains
        )
        if tick_index == 0:
            weight_totals = weight_grads
            vector_totals = vector_grads
        else:
            weight_totals = jax.tree.map(jnp.add, weight_totals, weight_grads)
            vector_totals = jax.tree.map(jnp.add, vector_totals, vector_grads)
        grad_low = grad_current.astype(jnp.bfloat16)
        backward_list.append(grad_low)
        returning = shifted(grad_low, "pipe", -1)
        kept_list.append(kept_state)
    summed = (
        lax.psum_scatter(
            weight_totals[0].astype(jnp.bfloat16), "dp", scatter_dimension=0, tiled=True
        ).astype(jnp.float32),
        lax.psum_scatter(
            weight_totals[1].astype(jnp.bfloat16), "dp", scatter_dimension=1, tiled=True
        ).astype(jnp.float32),
        lax.psum_scatter(
            weight_totals[2].astype(jnp.bfloat16), "dp", scatter_dimension=0, tiled=True
        ).astype(jnp.float32),
        lax.psum_scatter(
            weight_totals[3].astype(jnp.bfloat16), "dp", scatter_dimension=1, tiled=True
        ).astype(jnp.float32),
    )
    gain_grads, row_grads, local_grads, hidden_grads = vector_totals
    zero_index = jnp.zeros((), jnp.int32)
    placed = lax.dynamic_update_slice(
        jnp.zeros((2, model_width), jnp.float32), local_grads, (zero_index, column * width_local)
    )
    bias_full = jnp.concatenate([placed, row_grads], axis=0)
    hidden_full = lax.dynamic_update_slice(
        jnp.zeros((hidden_width,), jnp.float32), hidden_grads, (column * hidden_local,)
    )
    vector_sums = (
        lax.psum_scatter(gain_grads, ("dp", "tensor"), scatter_dimension=1, tiled=True),
        lax.psum_scatter(bias_full, ("dp", "tensor"), scatter_dimension=1, tiled=True),
        lax.psum_scatter(hidden_full, ("dp", "tensor"), scatter_dimension=0, tiled=True),
    )
    section_rows = jnp.stack(
        [
            jnp.where(section_first, forward_list[batch_index], forward_list[batch_index + 1])
            for batch_index in range(micro_count)
        ]
    )[None]
    grad_rows = jnp.stack(
        [
            jnp.where(section_first, backward_list[batch_index + 2], backward_list[batch_index + 1])
            for batch_index in range(micro_count)
        ]
    )[None]
    return (
        section_rows,
        grad_rows,
        summed[0][None],
        summed[1][None],
        summed[2][None],
        summed[3][None],
        vector_sums[0][None],
        vector_sums[1][None],
        vector_sums[2][None],
    )


def solution(mesh):
    return jax.shard_map(
        body,
        mesh=mesh,
        in_specs=(
            P(None, ("dp", "tensor"), None),
            P(None, "dp"),
            P(None, ("dp", "tensor"), None),
            P("pipe", "dp", None, "tensor"),
            P("pipe", "tensor", "dp"),
            P("pipe", "dp", "tensor"),
            P("pipe", "tensor", "dp"),
            P("pipe", None, None),
            P("pipe", None, None),
            P("pipe", None),
        ),
        out_specs=(
            P("pipe", None, ("dp", "tensor"), None),
            P("pipe", None, ("dp", "tensor"), None),
            P("pipe", "dp", None, "tensor"),
            P("pipe", "tensor", "dp"),
            P("pipe", "dp", "tensor"),
            P("pipe", "tensor", "dp"),
            P("pipe", None, ("dp", "tensor")),
            P("pipe", None, ("dp", "tensor")),
            P("pipe", ("dp", "tensor")),
        ),
        check_vma=False,
    )
```

profile of v0, /device:TPU:0, one launch (start us, length us, event | category | flops | bytes accessed | tf_op | source)
XLA Modules:
  0.0 1324.4 jit_solution(16337392418680728141)
XLA Ops:
  43.2 27.1 %reduce-scatter.35.cloned.1.call-done = f32[64,1024]{1,0:T(8,128)} async-done(((f32[256,1024]{1,0:T(8,128)}), f32[64,1024]{1,0:T(8,128)}) %reduce-scatter.35.cloned.1.call-update) | async-done | bytes 262160 | tf_op jit(solution)/shard_map/reduce_scatter | solution.py:136
  98.4 18.8 %all-gather.13.cloned.1.call-done = bf16[1,1024,1024]{2,1,0:T(8,128)(2,1)} async-done(((bf16[1,1024,256]{2,1,0:T(8,128)(2,1)}), bf16[1,1024,1024]{2,1,0:T(8,128)(2,1)}) %all-gather.13.cloned.1.call-update) | async-done | bytes 2097168 | tf_op jit(solution)/shard_map/all_gather | solution.py:254
  121.6 20.6 %reduce-scatter.37.cloned.1.call-done = bf16[64,1024]{1,0:T(8,128)(2,1)} async-done(((bf16[256,1024]{1,0:T(8,128)(2,1)}), bf16[64,1024]{1,0:T(8,128)(2,1)}) %reduce-scatter.37.cloned.1.call-update) | async-done | bytes 131088 | tf_op jit(solution)/shard_map/reduce_scatter | solution.py:144
  167.5 19.8 %reduce-scatter.55.cloned.1.call-done = bf16[64,1024]{1,0:T(8,128)(2,1)} async-done(((bf16[256,1024]{1,0:T(8,128)(2,1)}), bf16[64,1024]{1,0:T(8,128)(2,1)}) %reduce-scatter.55.cloned.1.call-update) | async-done | bytes 131088 | tf_op jit(solution)/shard_map/reduce_scatter | solution.py:192
  218.4 25.7 %reduce-scatter.39.cloned.1.call-done = f32[64,1024]{1,0:T(8,128)} async-done(((f32[256,1024]{1,0:T(8,128)}), f32[64,1024]{1,0:T(8,128)}) %reduce-scatter.39.cloned.1.call-update) | async-done | bytes 262160 | tf_op jit(solution)/shard_map/reduce_scatter | solution.py:136
  399.1 26.2 %reduce-scatter.43.cloned.1.call-done = f32[64,1024]{1,0:T(8,128)} async-done(((f32[256,1024]{1,0:T(8,128)}), f32[64,1024]{1,0:T(8,128)}) %reduce-scatter.43.cloned.1.call-update) | async-done | bytes 262160 | tf_op jit(solution)/shard_map/reduce_scatter | solution.py:136
  452.7 18.0 %all_gather.121 = bf16[256,1024]{1,0:T(8,128)(2,1)S(1)} all-gather(bf16[64,1024]{1,0:T(8,128)(2,1)S(1)} %convert_element_type.649), channel_id=1, replica_groups=mesh['pipe'=2,'dp'=4,'tensor'=4] {'tensor'}, dimensions={0}, use_global_device_ids=true | all-gather | bytes 655360 | tf_op jit(solution)/shard_map/all_gather | solution.py:196
  490.1 17.9 %all_gather.114 = bf16[256,1024]{1,0:T(8,128)(2,1)S(1)} all-gather(bf16[64,1024]{1,0:T(8,128)(2,1)S(1)} %bitcast_select_fusion.6), channel_id=1, replica_groups=mesh['pipe'=2,'dp'=4,'tensor'=4] {'tensor'}, dimensions={0}, use_global_device_ids=true | all-gather | bytes 655360 | tf_op jit(solution)/shard_map/all_gather | solution.py:129
  523.9 20.3 %all_gather.122 = bf16[256,1024]{1,0:T(8,128)(2,1)S(1)} all-gather(bf16[64,1024]{1,0:T(8,128)(2,1)S(1)} %get-tuple-element.384), channel_id=1, replica_groups=mesh['pipe'=2,'dp'=4,'tensor'=4] {'tensor'}, dimensions={0}, use_global_device_ids=true | all-gather | bytes 655360 | tf_op jit(solution)/shard_map/all_gather | solution.py:186
  551.2 20.7 %reduce-scatter.63.cloned.1.call-done = bf16[64,1024]{1,0:T(8,128)(2,1)} async-done(((bf16[256,1024]{1,0:T(8,128)(2,1)}), bf16[64,1024]{1,0:T(8,128)(2,1)}) %reduce-scatter.63.cloned.1.call-update) | async-done | bytes 131088 | tf_op jit(solution)/shard_map/reduce_scatter | solution.py:192
  596.4 20.2 %reduce-scatter.49.cloned.1.call-done = bf16[64,1024]{1,0:T(8,128)(2,1)} async-done(((bf16[256,1024]{1,0:T(8,128)(2,1)}), bf16[64,1024]{1,0:T(8,128)(2,1)}) %reduce-scatter.49.cloned.1.call-update) | async-done | bytes 131088 | tf_op jit(solution)/shard_map/reduce_scatter | solution.py:144
  645.1 27.3 %reduce-scatter.51.cloned.1.call-done = f32[64,1024]{1,0:T(8,128)} async-done(((f32[256,1024]{1,0:T(8,128)}), f32[64,1024]{1,0:T(8,128)}) %reduce-scatter.51.cloned.1.call-update) | async-done | bytes 262160 | tf_op jit(solution)/shard_map/reduce_scatter | solution.py:136
  698.4 18.1 %all_gather.123 = bf16[256,1024]{1,0:T(8,128)(2,1)S(1)} all-gather(bf16[64,1024]{1,0:T(8,128)(2,1)S(1)} %convert_element_type.661), channel_id=1, replica_groups=mesh['pipe'=2,'dp'=4,'tensor'=4] {'tensor'}, dimensions={0}, use_global_device_ids=true | all-gather | bytes 655360 | tf_op jit(solution)/shard_map/all_gather | solution.py:196
  736.3 17.8 %all_gather.128 = bf16[256,1024]{1,0:T(8,128)(2,1)S(1)} all-gather(bf16[64,1024]{1,0:T(8,128)(2,1)S(1)} %broadcast_select_fusion.9), channel_id=1, replica_groups=mesh['pipe'=2,'dp'=4,'tensor'=4] {'tensor'}, dimensions={0}, use_global_device_ids=true | all-gather | bytes 655360 | tf_op jit(solution)/shard_map/all_gather | solution.py:129
  769.7 21.1 %all_gather.124 = bf16[256,1024]{1,0:T(8,128)(2,1)S(1)} all-gather(bf16[64,1024]{1,0:T(8,128)(2,1)S(1)} %get-tuple-element.377), channel_id=1, replica_groups=mesh['pipe'=2,'dp'=4,'tensor'=4] {'tensor'}, dimensions={0}, use_global_device_ids=true | all-gather | bytes 655360 | tf_op jit(solution)/shard_map/all_gather | solution.py:186
  798.7 19.1 %reduce-scatter.67.cloned.1.call-done = bf16[64,1024]{1,0:T(8,128)(2,1)} async-done(((bf16[256,1024]{1,0:T(8,128)(2,1)}), bf16[64,1024]{1,0:T(8,128)(2,1)}) %reduce-scatter.67.cloned.1.call-update) | async-done | bytes 131088 | tf_op jit(solution)/shard_map/reduce_scatter | solution.py:192
  847.5 18.1 %all_gather.129 = bf16[256,1024]{1,0:T(8,128)(2,1)S(1)} all-gather(bf16[64,1024]{1,0:T(8,128)(2,1)} %get-tuple-element.464), channel_id=1, replica_groups=mesh['pipe'=2,'dp'=4,'tensor'=4] {'tensor'}, dimensions={0}, use_global_device_ids=true | all-gather | bytes 655360 | tf_op jit(solution)/shard_map/all_gather | solution.py:140
  881.6 20.7 %all_gather.126 = bf16[256,1024]{1,0:T(8,128)(2,1)S(1)} all-gather(bf16[64,1024]{1,0:T(8,128)(2,1)S(1)} %get-tuple-element.370), channel_id=1, replica_groups=mesh['pipe'=2,'dp'=4,'tensor'=4] {'tensor'}, dimensions={0}, use_global_device_ids=true | all-gather | bytes 655360 | tf_op jit(solution)/shard_map/all_gather | solution.py:186
  1102.5 58.1 %all-reduce = f32[4096]{0:T(1024)S(1)} all-reduce(f32[4096]{0:T(1024)S(1)} %add_dynamic-update-slice_fusion), channel_id=37, replica_groups=mesh['pipe'=2,'dp'=4,'tensor'=4] {'dp','tensor'}, use_global_device_ids=true, to_apply=%region_143.144.clone | all-reduce | flops 4096 | bytes 32768
  1172.3 22.4 %reduce-scatter.81.cloned.1.call-done = bf16[64,1024]{1,0:T(8,128)(2,1)} async-done(((bf16[256,1024]{1,0:T(8,128)(2,1)}), bf16[64,1024]{1,0:T(8,128)(2,1)}) %reduce-scatter.81.cloned.1.call-update) | async-done | bytes 131088 | tf_op jit(solution)/shard_map/reduce_scatter | solution.py:206
  1196.5 21.0 %reduce-scatter.85.cloned.1.call-done = bf16[256,256]{1,0:T(8,128)(2,1)} async-done(((bf16[256,1024]{1,0:T(8,128)(2,1)}), bf16[256,256]{1,0:T(8,128)(2,1)}) %reduce-scatter.85.cloned.1.call-update) | async-done | bytes 131088 | tf_op jit(solution)/shard_map/reduce_scatter | solution.py:296
  1219.1 32.1 %reduce-scatter.87.cloned.1.call-done = bf16[256,1024]{1,0:T(8,128)(2,1)} async-done(((bf16[1024,1024]{1,0:T(8,128)(2,1)}), bf16[256,1024]{1,0:T(8,128)(2,1)}) %reduce-scatter.87.cloned.1.call-update) | async-done | bytes 524304 | tf_op jit(solution)/shard_map/reduce_scatter | solution.py:299
  1253.3 31.6 %reduce-scatter.89.cloned.1.call-done = bf16[1024,256]{1,0:T(8,128)(2,1)} async-done(((bf16[1024,1024]{1,0:T(8,128)(2,1)}), bf16[1024,256]{1,0:T(8,128)(2,1)}) %reduce-scatter.89.cloned.1.call-update) | async-done | bytes 524304 | tf_op jit(solution)/shard_map/reduce_scatter | solution.py:302
  1287.0 28.4 %reduce-scatter.83.cloned.1.call-done = bf16[256,3,256]{2,0,1:T(8,128)(2,1)} async-done(((bf16[1024,3,256]{2,0,1:T(8,128)(2,1)}), bf16[256,3,256]{2,0,1:T(8,128)(2,1)}) %reduce-scatter.83.cloned.1.call-update) | async-done | bytes 393232 | tf_op jit(solution)/shard_map/reduce_scatter | solution.py:293
  (1219 shorter events, 733.2 us)
Async XLA Ops:
  42.5 74.7 %all-gather.13.cloned.1.call-start = ((), (), s32[]{:S(2)}) async-start(), calls=%async_computation.60 | async-start | bytes 2621440 | tf_op jit(solution)/shard_map/all_gather | solution.py:254
  43.1 99.2 %reduce-scatter.37.cloned.1.call-start = ((), (), s32[]{:S(2)}) async-start(), calls=%async_computation.31 | async-start | bytes 655360 | tf_op jit(solution)/shard_map/reduce_scatter | solution.py:144
  120.3 66.9 %reduce-scatter.55.cloned.1.call-start = ((), (), s32[]{:S(2)}) async-start(), calls=%async_computation.40 | async-start | bytes 655360 | tf_op jit(solution)/shard_map/reduce_scatter | solution.py:192
  166.8 77.3 %reduce-scatter.39.cloned.1.call-start = ((), (), s32[]{:S(2)}) async-start(), calls=%async_computation.32 | async-start | bytes 1310720 | tf_op jit(solution)/shard_map/reduce_scatter | solution.py:136
  216.7 94.3 %reduce-scatter.41.cloned.1.call-start = ((), (), s32[]{:S(2)}) async-start(), calls=%async_computation.33 | async-start | bytes 655360 | tf_op jit(solution)/shard_map/reduce_scatter | solution.py:144
  297.9 99.6 %reduce-scatter.59.cloned.1.call-start = ((), (), s32[]{:S(2)}) async-start(), calls=%async_computation.42 | async-start | bytes 655360 | tf_op jit(solution)/shard_map/reduce_scatter | solution.py:192
  383.9 95.0 %reduce-scatter.45.cloned.1.call-start = ((), (), s32[]{:S(2)}) async-start(), calls=%async_computation.35 | async-start | bytes 655360 | tf_op jit(solution)/shard_map/reduce_scatter | solution.py:144
  451.6 61.8 %reduce-scatter.61.cloned.1.call-start = ((), (), s32[]{:S(2)}) async-start(), calls=%async_computation.43 | async-start | bytes 655360 | tf_op jit(solution)/shard_map/reduce_scatter | solution.py:206
  488.1 61.8 %reduce-scatter.47.cloned.1.call-start = ((), (), s32[]{:S(2)}) async-start(), calls=%async_computation.36 | async-start | bytes 1310720 | tf_op jit(solution)/shard_map/reduce_scatter | solution.py:136
  549.8 66.8 %reduce-scatter.49.cloned.1.call-start = ((), (), s32[]{:S(2)}) async-start(), calls=%async_computation.37 | async-start | bytes 655360 | tf_op jit(solution)/shard_map/reduce_scatter | solution.py:144
  596.1 76.3 %reduce-scatter.51.cloned.1.call-start = ((), (), s32[]{:S(2)}) async-start(), calls=%async_computation.38 | async-start | bytes 1310720 | tf_op jit(solution)/shard_map/reduce_scatter | solution.py:136
  645.0 82.0 %reduce-scatter.53.cloned.1.call-start = ((), (), s32[]{:S(2)}) async-start(), calls=%async_computation.39 | async-start | bytes 655360 | tf_op jit(solution)/shard_map/reduce_scatter | solution.py:144
  734.6 61.5 %reduce-scatter.75.cloned.1.call-start = ((), (), s32[]{:S(2)}) async-start(), calls=%async_computation.50 | async-start | bytes 1310720 | tf_op jit(solution)/shard_map/reduce_scatter | solution.py:136
  794.2 75.0 %reduce-scatter.69.cloned.1.call-start = ((), (), s32[]{:S(2)}) async-start(), calls=%async_computation.47 | async-start | bytes 655360 | tf_op jit(solution)/shard_map/reduce_scatter | solution.py:206
  846.8 71.2 %reduce-scatter.77.cloned.1.call-start = ((), (), s32[]{:S(2)}) async-start(), calls=%async_computation.51 | async-start | bytes 655360 | tf_op jit(solution)/shard_map/reduce_scatter | solution.py:144
  908.5 74.3 %reduce-scatter.73.cloned.1.call-start = ((), (), s32[]{:S(2)}) async-start(), calls=%async_computation.49 | async-start | bytes 655360 | tf_op jit(solution)/shard_map/reduce_scatter | solution.py:206
  962.4 71.3 %reduce-scatter.79.cloned.1.call-start = ((), (), s32[]{:S(2)}) async-start(), calls=%async_computation.52 | async-start | bytes 655360 | tf_op jit(solution)/shard_map/reduce_scatter | solution.py:192
  1013.7 147.5 %reduce-scatter.91.cloned.1.call-start = ((), (), s32[]{:S(2)}) async-start(), calls=%async_computation.61 | async-start | bytes 557056
  1057.3 113.6 %reduce-scatter.93.cloned.1.call-start = ((), (), s32[]{:S(2)}) async-start(), calls=%async_computation.62 | async-start | bytes 557056
  1060.2 134.4 %reduce-scatter.81.cloned.1.call-start = ((), (), s32[]{:S(2)}) async-start(), calls=%async_computation.53 | async-start | bytes 655360 | tf_op jit(solution)/shard_map/reduce_scatter | solution.py:206
  1062.8 154.7 %reduce-scatter.85.cloned.1.call-start = ((), (), s32[]{:S(2)}) async-start(), calls=%async_computation.55 | async-start | bytes 655360 | tf_op jit(solution)/shard_map/reduce_scatter | solution.py:296
  1069.9 181.3 %reduce-scatter.87.cloned.1.call-start = ((), (), s32[]{:S(2)}) async-start(), calls=%async_computation.56 | async-start | bytes 2621440 | tf_op jit(solution)/shard_map/reduce_scatter | solution.py:299
  1080.0 204.9 %reduce-scatter.89.cloned.1.call-start = ((), (), s32[]{:S(2)}) async-start(), calls=%async_computation.57 | async-start | bytes 2621440 | tf_op jit(solution)/shard_map/reduce_scatter | solution.py:302
  1091.6 223.8 %reduce-scatter.83.cloned.1.call-start = ((), (), s32[]{:S(2)}) async-start(), calls=%async_computation.54 | async-start | bytes 1966080 | tf_op jit(solution)/shard_map/reduce_scatter | solution.py:293
  (400 other events, 4967.2 us)
Sparse Core Ops, SparseCore 0:
  10.1 22.6 all-gather.8
  41.9 28.3 reduce-scatter.34
  71.8 21.0 all-gather.10
  94.3 22.8 all-gather.12
  120.4 21.8 reduce-scatter.36
  216.8 27.2 reduce-scatter.38
  376.9 20.5 reduce-scatter.58
  399.8 25.5 reduce-scatter.42
  451.7 22.2 reduce-scatter.44
  488.2 21.2 reduce-scatter.60
  513.5 35.2 reduce-scatter.46
  645.2 27.2 reduce-scatter.50
  698.4 21.8 reduce-scatter.52
  734.7 21.0 reduce-scatter.64
  758.6 35.9 reduce-scatter.74
  846.9 22.0 reduce-scatter.68
  877.9 25.8 reduce-scatter.76
  908.6 22.3 reduce-scatter.70
  1057.4 54.6 reduce-scatter.90
  1115.6 55.2 reduce-scatter.92
  1173.7 20.8 reduce-scatter.80
  1220.0 31.1 reduce-scatter.86
  1253.7 31.1 reduce-scatter.88
  1287.3 28.0 reduce-scatter.82
  (9 shorter events, 181.0 us)
where the time goes:
time: 1340 us; the launch traced here: 1320 us
  waiting for transfers between devices  477 us (36%)
  blocking collectives  467 us (35%)
  matrix products  163 us (12%)
  other arithmetic  113 us (8%)
  local copies, waits for them, and re-layouts  58.1 us (4%)
  starting transfers between devices  25.9 us (2%)
  between operations  20.3 us (2%)
    all_gather x6, blocking collectives, layer_backward(): lax.all_gather(grad_second.astype(jnp.bfloat16), 'tensor', axis=0, tiled=...  108 us
    reduce_scatter x6, waiting for transfers between devices, layer_forward(): lax.psum_scatter(partial_value, 'tensor', scatter_dimension=0, tiled=True)  106 us
    reduce_scatter x6, waiting for transfers between devices, layer_backward(): lax.psum_scatter(grad_spread.astype(jnp.bfloat16), 'tensor', scatter_dime...  98.7 us
    all_gather x6, blocking collectives, layer_backward(): lax.all_gather(grad_first.astype(jnp.bfloat16), 'tensor', axis=0, tiled=T...  98.5 us
    all_gather x6, blocking collectives, layer_forward(): gathered = lax.all_gather(current, 'tensor', axis=0, tiled=True)  97.8 us
    all_gather x6, blocking collectives, layer_forward(): lax.all_gather(normed.astype(jnp.bfloat16), 'tensor', axis=0, tiled=True)  97 us
    unnamed x1, blocking collectives  58.1 us
    reduce_scatter x6, waiting for transfers between devices, layer_forward(): lax.psum_scatter(partial_out.astype(jnp.bfloat16), 'tensor', scatter_dime...  54 us
  transfers between devices with their start and end apart: 43, of which 31 were waited for; matrix products, arithmetic and copies ran while one was open for 13% of the time, Pallas kernels for 0%

commit v1 on v0

--- a/solution.py
+++ b/solution.py
@@ -126,7 +126,23 @@
 def layer_forward(current, labels, weights, vectors):
     w_qkv, w_o, w_in, w_out = weights
     gains, biases, query_bias, value_bias, local_hidden_bias = vectors
-    gathered = lax.all_gather(current, "tensor", axis=0, tiled=True)
+    size, place, span = (lax.axis_size("tensor"), lax.axis_index("tensor"), current.shape[0])
+    right = [(i_2, (i_2 + 1) % size) for i_2 in range(size)]
+    left = [(i_2, (i_2 - 1) % size) for i_2 in range(size)]
+    gathered = jnp.zeros((*current.shape[:0], size * span, *current.shape[0 + 1 :]), current.dtype)
+    gathered = lax.dynamic_update_slice_in_dim(gathered, current, place * span, axis=0)
+    from_left = from_right = current
+    middle = size // 2
+    for step in range(1, middle + 1):
+        from_left = lax.ppermute(from_left, "tensor", right)
+        gathered = lax.dynamic_update_slice_in_dim(
+            gathered, from_left, (place - step) % size * span, axis=0
+        )
+        if step < size - middle:
+            from_right = lax.ppermute(from_right, "tensor", left)
+            gathered = lax.dynamic_update_slice_in_dim(
+                gathered, from_right, (place + step) % size * span, axis=0
+            )
     projected = jnp.einsum("gd,dcn->gcn", gathered, w_qkv, preferred_element_type=jnp.float32)
     queries = (projected[:, 0] + query_bias).astype(jnp.bfloat16)
     key_rows = projected[:, 1].astype(jnp.bfloat16)

time: 1340 us -> 1320 us (0.985)
  blocking collectives: 467 us -> 371 us
  waiting for transfers between devices: 477 us -> 534 us
  starting transfers between devices: 25.9 us -> 51.8 us
    all_gather x6 -> x0, blocking collectives: 97.8 us -> none  [layer_forward(): gathered = lax.all_gather(current, 'tensor', axis=0, tiled=True)]
    ppermute x0 -> x18, waiting for transfers between devices: none -> 44.7 us  [the longest x12 44.7 us: layer_forward(): from_left = lax.ppermute(from_left, 'tensor', right)]
    ppermute x0 -> x18, starting transfers between devices: none -> 24.9 us  [the longest x6 21.2 us: layer_forward(): from_right = lax.ppermute(from_right, 'tensor', left)]
    reduce_scatter x6, waiting for transfers between devices: 51.7 us -> 68.2 us  [layer_backward(): lax.psum_scatter(grad_gathered.astype(jnp.bfloat16), 'tensor', scatter_di...]
    unnamed x770 -> x836, local copies, waits for them, and re-layouts: 39.2 us -> 39.3 us
  transfers between devices with their start and end apart: 43 -> 61, of which waited for: 31 -> 45; matrix products, arithmetic and copies ran while one was open for 13% -> 14% of each run, Pallas kernels for 0% -> 0%
where the time goes in v1:
time: 1320 us; the launch traced here: 1310 us
  waiting for transfers between devices  534 us (40%)
  blocking collectives  371 us (28%)
  matrix products  161 us (12%)
  other arithmetic  110 us (8%)
  local copies, waits for them, and re-layouts  62.5 us (5%)
  starting transfers between devices  51.8 us (4%)
  between operations  21 us (2%)
    all_gather x6, blocking collectives, layer_backward(): lax.all_gather(grad_second.astype(jnp.bfloat16), 'tensor', axis=0, tiled=...  108 us
    reduce_scatter x6, waiting for transfers between devices, layer_forward(): lax.psum_scatter(partial_value, 'tensor', scatter_dimension=0, tiled=True)  101 us
    all_gather x6, blocking collectives, layer_backward(): lax.all_gather(grad_first.astype(jnp.bfloat16), 'tensor', axis=0, tiled=T...  98.8 us
    reduce_scatter x6, waiting for transfers between devices, layer_backward(): lax.psum_scatter(grad_spread.astype(jnp.bfloat16), 'tensor', scatter_dime...  97.7 us
    all_gather x6, blocking collectives, layer_forward(): lax.all_gather(normed.astype(jnp.bfloat16), 'tensor', axis=0, tiled=True)  97.2 us
    reduce_scatter x6, waiting for transfers between devices, layer_backward(): lax.psum_scatter(grad_gathered.astype(jnp.bfloat16), 'tensor', scatter_di...  68.2 us
    unnamed x1, blocking collectives  58.2 us
    reduce_scatter x6, waiting for transfers between devices, layer_forward(): lax.psum_scatter(partial_out.astype(jnp.bfloat16), 'tensor', scatter_dime...  54.1 us
  transfers between devices with their start and end apart: 61, of which 45 were waited for; matrix products, arithmetic and copies ran while one was open for 14% of the time, Pallas kernels for 0%

profile of v1, /device:TPU:0, one launch (start us, length us, event | category | flops | bytes accessed | tf_op | source)
XLA Modules:
  0.0 1310.7 jit_solution(2642033085589980787)
XLA Ops:
  39.5 25.3 %reduce-scatter.35.cloned.1.call-done = f32[64,1024]{1,0:T(8,128)} async-done(((f32[256,1024]{1,0:T(8,128)}), f32[64,1024]{1,0:T(8,128)}) %reduce-scatter.35.cloned.1.call-update) | async-done | bytes 262160 | tf_op jit(solution)/shard_map/reduce_scatter | solution.py:152
  92.9 18.8 %all-gather.12.cloned.1.call-done = bf16[1,1024,1024]{2,1,0:T(8,128)(2,1)} async-done(((bf16[1,1024,256]{2,1,0:T(8,128)(2,1)}), bf16[1,1024,1024]{2,1,0:T(8,128)(2,1)}) %all-gather.12.cloned.1.call-update) | async-done | bytes 2097168 | tf_op jit(solution)/shard_map/all_gather | solution.py:270
  116.1 20.7 %reduce-scatter.37.cloned.1.call-done = bf16[64,1024]{1,0:T(8,128)(2,1)} async-done(((bf16[256,1024]{1,0:T(8,128)(2,1)}), bf16[64,1024]{1,0:T(8,128)(2,1)}) %reduce-scatter.37.cloned.1.call-update) | async-done | bytes 131088 | tf_op jit(solution)/shard_map/reduce_scatter | solution.py:160
  161.3 20.4 %reduce-scatter.55.cloned.1.call-done = bf16[64,1024]{1,0:T(8,128)(2,1)} async-done(((bf16[256,1024]{1,0:T(8,128)(2,1)}), bf16[64,1024]{1,0:T(8,128)(2,1)}) %reduce-scatter.55.cloned.1.call-update) | async-done | bytes 131088 | tf_op jit(solution)/shard_map/reduce_scatter | solution.py:208
  212.2 25.3 %reduce-scatter.39.cloned.1.call-done = f32[64,1024]{1,0:T(8,128)} async-done(((f32[256,1024]{1,0:T(8,128)}), f32[64,1024]{1,0:T(8,128)}) %reduce-scatter.39.cloned.1.call-update) | async-done | bytes 262160 | tf_op jit(solution)/shard_map/reduce_scatter | solution.py:152
  242.9 16.1 %all_gather.96 = bf16[256,1024]{1,0:T(8,128)(2,1)S(1)} all-gather(bf16[64,1024]{1,0:T(8,128)(2,1)S(1)} %convert_element_type.638), channel_id=1, replica_groups=mesh['pipe'=2,'dp'=4,'tensor'=4] {'tensor'}, dimensions={0}, use_global_device_ids=true | all-gather | bytes 655360 | tf_op jit(solution)/shard_map/all_gather | solution.py:212
  311.2 16.4 %reduce-scatter.57.cloned.1.call-done = bf16[64,1024]{1,0:T(8,128)(2,1)} async-done(((bf16[256,1024]{1,0:T(8,128)(2,1)}), bf16[64,1024]{1,0:T(8,128)(2,1)}) %reduce-scatter.57.cloned.1.call-update) | async-done | bytes 131088 | tf_op jit(solution)/shard_map/reduce_scatter | solution.py:222
  380.2 26.3 %reduce-scatter.43.cloned.1.call-done = f32[64,1024]{1,0:T(8,128)} async-done(((f32[256,1024]{1,0:T(8,128)}), f32[64,1024]{1,0:T(8,128)}) %reduce-scatter.43.cloned.1.call-update) | async-done | bytes 262160 | tf_op jit(solution)/shard_map/reduce_scatter | solution.py:152
  434.0 17.9 %all_gather.98 = bf16[256,1024]{1,0:T(8,128)(2,1)S(1)} all-gather(bf16[64,1024]{1,0:T(8,128)(2,1)S(1)} %convert_element_type.649), channel_id=1, replica_groups=mesh['pipe'=2,'dp'=4,'tensor'=4] {'tensor'}, dimensions={0}, use_global_device_ids=true | all-gather | bytes 655360 | tf_op jit(solution)/shard_map/all_gather | solution.py:212
  508.9 21.1 %all_gather.99 = bf16[256,1024]{1,0:T(8,128)(2,1)S(1)} all-gather(bf16[64,1024]{1,0:T(8,128)(2,1)S(1)} %get-tuple-element.386), channel_id=1, replica_groups=mesh['pipe'=2,'dp'=4,'tensor'=4] {'tensor'}, dimensions={0}, use_global_device_ids=true | all-gather | bytes 655360 | tf_op jit(solution)/shard_map/all_gather | solution.py:202
  537.0 20.9 %reduce-scatter.63.cloned.1.call-done = bf16[64,1024]{1,0:T(8,128)(2,1)} async-done(((bf16[256,1024]{1,0:T(8,128)(2,1)}), bf16[64,1024]{1,0:T(8,128)(2,1)}) %reduce-scatter.63.cloned.1.call-update) | async-done | bytes 131088 | tf_op jit(solution)/shard_map/reduce_scatter | solution.py:208
  582.7 20.3 %reduce-scatter.49.cloned.1.call-done = bf16[64,1024]{1,0:T(8,128)(2,1)} async-done(((bf16[256,1024]{1,0:T(8,128)(2,1)}), bf16[64,1024]{1,0:T(8,128)(2,1)}) %reduce-scatter.49.cloned.1.call-update) | async-done | bytes 131088 | tf_op jit(solution)/shard_map/reduce_scatter | solution.py:160
  632.6 24.2 %reduce-scatter.51.cloned.1.call-done = f32[64,1024]{1,0:T(8,128)} async-done(((f32[256,1024]{1,0:T(8,128)}), f32[64,1024]{1,0:T(8,128)}) %reduce-scatter.51.cloned.1.call-update) | async-done | bytes 262160 | tf_op jit(solution)/shard_map/reduce_scatter | solution.py:152
  683.4 18.1 %all_gather.100 = bf16[256,1024]{1,0:T(8,128)(2,1)S(1)} all-gather(bf16[64,1024]{1,0:T(8,128)(2,1)S(1)} %convert_element_type.661), channel_id=1, replica_groups=mesh['pipe'=2,'dp'=4,'tensor'=4] {'tensor'}, dimensions={0}, use_global_device_ids=true | all-gather | bytes 655360 | tf_op jit(solution)/shard_map/all_gather | solution.py:212
  757.8 21.1 %all_gather.101 = bf16[256,1024]{1,0:T(8,128)(2,1)S(1)} all-gather(bf16[64,1024]{1,0:T(8,128)(2,1)S(1)} %get-tuple-element.379), channel_id=1, replica_groups=mesh['pipe'=2,'dp'=4,'tensor'=4] {'tensor'}, dimensions={0}, use_global_device_ids=true | all-gather | bytes 655360 | tf_op jit(solution)/shard_map/all_gather | solution.py:202
  785.9 20.8 %reduce-scatter.67.cloned.1.call-done = bf16[64,1024]{1,0:T(8,128)(2,1)} async-done(((bf16[256,1024]{1,0:T(8,128)(2,1)}), bf16[64,1024]{1,0:T(8,128)(2,1)}) %reduce-scatter.67.cloned.1.call-update) | async-done | bytes 131088 | tf_op jit(solution)/shard_map/reduce_scatter | solution.py:208
  835.6 18.1 %all_gather.105 = bf16[256,1024]{1,0:T(8,128)(2,1)S(1)} all-gather(bf16[64,1024]{1,0:T(8,128)(2,1)} %get-tuple-element.476), channel_id=1, replica_groups=mesh['pipe'=2,'dp'=4,'tensor'=4] {'tensor'}, dimensions={0}, use_global_device_ids=true | all-gather | bytes 655360 | tf_op jit(solution)/shard_map/all_gather | solution.py:156
  869.5 21.0 %all_gather.103 = bf16[256,1024]{1,0:T(8,128)(2,1)S(1)} all-gather(bf16[64,1024]{1,0:T(8,128)(2,1)S(1)} %get-tuple-element.372), channel_id=1, replica_groups=mesh['pipe'=2,'dp'=4,'tensor'=4] {'tensor'}, dimensions={0}, use_global_device_ids=true | all-gather | bytes 655360 | tf_op jit(solution)/shard_map/all_gather | solution.py:202
  1087.8 58.2 %all-reduce = f32[4096]{0:T(1024)S(1)} all-reduce(f32[4096]{0:T(1024)S(1)} %add_dynamic-update-slice_fusion), channel_id=36, replica_groups=mesh['pipe'=2,'dp'=4,'tensor'=4] {'dp','tensor'}, use_global_device_ids=true, to_apply=%region_143.144.clone | all-reduce | flops 4096 | bytes 32768
  1158.6 22.3 %reduce-scatter.81.cloned.1.call-done = bf16[64,1024]{1,0:T(8,128)(2,1)} async-done(((bf16[256,1024]{1,0:T(8,128)(2,1)}), bf16[64,1024]{1,0:T(8,128)(2,1)}) %reduce-scatter.81.cloned.1.call-update) | async-done | bytes 131088 | tf_op jit(solution)/shard_map/reduce_scatter | solution.py:222
  1182.8 21.0 %reduce-scatter.85.cloned.1.call-done = bf16[256,256]{1,0:T(8,128)(2,1)} async-done(((bf16[256,1024]{1,0:T(8,128)(2,1)}), bf16[256,256]{1,0:T(8,128)(2,1)}) %reduce-scatter.85.cloned.1.call-update) | async-done | bytes 131088 | tf_op jit(solution)/shard_map/reduce_scatter | solution.py:312
  1205.5 32.1 %reduce-scatter.87.cloned.1.call-done = bf16[256,1024]{1,0:T(8,128)(2,1)} async-done(((bf16[1024,1024]{1,0:T(8,128)(2,1)}), bf16[256,1024]{1,0:T(8,128)(2,1)}) %reduce-scatter.87.cloned.1.call-update) | async-done | bytes 524304 | tf_op jit(solution)/shard_map/reduce_scatter | solution.py:315
  1239.7 31.6 %reduce-scatter.89.cloned.1.call-done = bf16[1024,256]{1,0:T(8,128)(2,1)} async-done(((bf16[1024,1024]{1,0:T(8,128)(2,1)}), bf16[1024,256]{1,0:T(8,128)(2,1)}) %reduce-scatter.89.cloned.1.call-update) | async-done | bytes 524304 | tf_op jit(solution)/shard_map/reduce_scatter | solution.py:318
  1273.4 28.4 %reduce-scatter.83.cloned.1.call-done = bf16[256,3,256]{2,0,1:T(8,128)(2,1)} async-done(((bf16[1024,3,256]{2,0,1:T(8,128)(2,1)}), bf16[256,3,256]{2,0,1:T(8,128)(2,1)}) %reduce-scatter.83.cloned.1.call-update) | async-done | bytes 393232 | tf_op jit(solution)/shard_map/reduce_scatter | solution.py:309
  (1339 shorter events, 723.2 us)
Async XLA Ops:
  38.8 72.9 %all-gather.12.cloned.1.call-start = ((), (), s32[]{:S(2)}) async-start(), calls=%async_computation.60 | async-start | bytes 2621440 | tf_op jit(solution)/shard_map/all_gather | solution.py:270
  39.4 97.4 %reduce-scatter.37.cloned.1.call-start = ((), (), s32[]{:S(2)}) async-start(), calls=%async_computation.31 | async-start | bytes 655360 | tf_op jit(solution)/shard_map/reduce_scatter | solution.py:160
  114.8 66.9 %reduce-scatter.55.cloned.1.call-start = ((), (), s32[]{:S(2)}) async-start(), calls=%async_computation.40 | async-start | bytes 655360 | tf_op jit(solution)/shard_map/reduce_scatter | solution.py:208
  161.3 76.2 %reduce-scatter.39.cloned.1.call-start = ((), (), s32[]{:S(2)}) async-start(), calls=%async_computation.32 | async-start | bytes 1310720 | tf_op jit(solution)/shard_map/reduce_scatter | solution.py:152
  211.0 93.6 %reduce-scatter.41.cloned.1.call-start = ((), (), s32[]{:S(2)}) async-start(), calls=%async_computation.33 | async-start | bytes 655360 | tf_op jit(solution)/shard_map/reduce_scatter | solution.py:160
  291.5 87.1 %reduce-scatter.59.cloned.1.call-start = ((), (), s32[]{:S(2)}) async-start(), calls=%async_computation.42 | async-start | bytes 655360 | tf_op jit(solution)/shard_map/reduce_scatter | solution.py:208
  369.2 90.2 %reduce-scatter.45.cloned.1.call-start = ((), (), s32[]{:S(2)}) async-start(), calls=%async_computation.35 | async-start | bytes 655360 | tf_op jit(solution)/shard_map/reduce_scatter | solution.py:160
  432.9 65.7 %reduce-scatter.61.cloned.1.call-start = ((), (), s32[]{:S(2)}) async-start(), calls=%async_computation.43 | async-start | bytes 655360 | tf_op jit(solution)/shard_map/reduce_scatter | solution.py:222
  490.6 67.3 %reduce-scatter.63.cloned.1.call-start = ((), (), s32[]{:S(2)}) async-start(), calls=%async_computation.44 | async-start | bytes 655360 | tf_op jit(solution)/shard_map/reduce_scatter | solution.py:208
  535.6 67.4 %reduce-scatter.49.cloned.1.call-start = ((), (), s32[]{:S(2)}) async-start(), calls=%async_computation.37 | async-start | bytes 655360 | tf_op jit(solution)/shard_map/reduce_scatter | solution.py:160
  582.6 74.2 %reduce-scatter.51.cloned.1.call-start = ((), (), s32[]{:S(2)}) async-start(), calls=%async_computation.38 | async-start | bytes 1310720 | tf_op jit(solution)/shard_map/reduce_scatter | solution.py:152
  630.3 80.3 %reduce-scatter.53.cloned.1.call-start = ((), (), s32[]{:S(2)}) async-start(), calls=%async_computation.39 | async-start | bytes 655360 | tf_op jit(solution)/shard_map/reduce_scatter | solution.py:160
  738.0 68.7 %reduce-scatter.67.cloned.1.call-start = ((), (), s32[]{:S(2)}) async-start(), calls=%async_computation.46 | async-start | bytes 655360 | tf_op jit(solution)/shard_map/reduce_scatter | solution.py:208
  783.0 74.1 %reduce-scatter.69.cloned.1.call-start = ((), (), s32[]{:S(2)}) async-start(), calls=%async_computation.47 | async-start | bytes 655360 | tf_op jit(solution)/shard_map/reduce_scatter | solution.py:222
  835.0 71.3 %reduce-scatter.77.cloned.1.call-start = ((), (), s32[]{:S(2)}) async-start(), calls=%async_computation.51 | async-start | bytes 655360 | tf_op jit(solution)/shard_map/reduce_scatter | solution.py:160
  896.8 72.8 %reduce-scatter.73.cloned.1.call-start = ((), (), s32[]{:S(2)}) async-start(), calls=%async_computation.49 | async-start | bytes 655360 | tf_op jit(solution)/shard_map/reduce_scatter | solution.py:222
  949.3 71.1 %reduce-scatter.79.cloned.1.call-start = ((), (), s32[]{:S(2)}) async-start(), calls=%async_computation.52 | async-start | bytes 655360 | tf_op jit(solution)/shard_map/reduce_scatter | solution.py:208
  1000.5 146.2 %reduce-scatter.91.cloned.1.call-start = ((), (), s32[]{:S(2)}) async-start(), calls=%async_computation.61 | async-start | bytes 557056
  1043.5 113.7 %reduce-scatter.93.cloned.1.call-start = ((), (), s32[]{:S(2)}) async-start(), calls=%async_computation.62 | async-start | bytes 557056
  1046.4 134.5 %reduce-scatter.81.cloned.1.call-start = ((), (), s32[]{:S(2)}) async-start(), calls=%async_computation.53 | async-start | bytes 655360 | tf_op jit(solution)/shard_map/reduce_scatter | solution.py:222
  1047.9 155.9 %reduce-scatter.85.cloned.1.call-start = ((), (), s32[]{:S(2)}) async-start(), calls=%async_computation.55 | async-start | bytes 655360 | tf_op jit(solution)/shard_map/reduce_scatter | solution.py:312
  1055.2 182.4 %reduce-scatter.87.cloned.1.call-start = ((), (), s32[]{:S(2)}) async-start(), calls=%async_computation.56 | async-start | bytes 2621440 | tf_op jit(solution)/shard_map/reduce_scatter | solution.py:315
  1065.3 206.0 %reduce-scatter.89.cloned.1.call-start = ((), (), s32[]{:S(2)}) async-start(), calls=%async_computation.57 | async-start | bytes 2621440 | tf_op jit(solution)/shard_map/reduce_scatter | solution.py:318
  1076.8 224.9 %reduce-scatter.83.cloned.1.call-start = ((), (), s32[]{:S(2)}) async-start(), calls=%async_computation.54 | async-start | bytes 1966080 | tf_op jit(solution)/shard_map/reduce_scatter | solution.py:309
  (451 other events, 5399.8 us)
Sparse Core Ops, SparseCore 0:
  10.2 23.2 all-gather.7
  38.2 26.5 reduce-scatter.34
  66.3 21.0 all-gather.9
  88.8 22.8 all-gather.11
  114.9 21.8 reduce-scatter.36
  211.1 26.3 reduce-scatter.38
  357.6 20.9 reduce-scatter.58
  380.9 25.5 reduce-scatter.42
  433.0 22.2 reduce-scatter.44
  477.6 20.9 reduce-scatter.60
  500.7 34.0 reduce-scatter.46
  630.4 26.4 reduce-scatter.50
  683.4 21.8 reduce-scatter.52
  724.7 21.9 reduce-scatter.64
  748.9 34.5 reduce-scatter.74
  835.1 22.0 reduce-scatter.68
  865.9 25.9 reduce-scatter.76
  896.9 22.6 reduce-scatter.70
  1043.6 54.6 reduce-scatter.90
  1101.8 55.2 reduce-scatter.92
  1160.0 20.8 reduce-scatter.80
  1206.4 31.1 reduce-scatter.86
  1240.1 31.1 reduce-scatter.88
  1273.7 28.0 reduce-scatter.82
  (9 shorter events, 180.9 us)
